TPU v7x, 512 devices: a whole 4x8x8 slice. The times are simulated.
512 devices in a mesh: gx: 32 (over x, z), gy: 16 (over y, core).
Axes of the slice: x: 4, y: 8, z: 8, core: 2. Of those that a mesh axis runs over, the one named last changes fastest.
Arguments:
- seeds: int32 [64, 1024], P('gy', 'gx'), may hold values from 0 to 1073741823
- lengths: float32 [3], replicated, may hold values from 3 to 24
- exponents: float32 [3], replicated, may hold values from 1.5 to 2.5
- storage: float32 [64, 1024, 1024], P('gy', 'gx'), may hold values from 0.5 to 8
- recharge: float32 [64, 1024, 1024], P('gy', 'gx'), may hold values from -36 to 36
- well_cells: int32 [3, 256], replicated, may hold values from 0 to 1023, as said below
- well_rates: float32 [256], replicated, may hold values from -180 to 180
Outputs:
- log_perm: float32 [64, 1024, 1024], P('gy', 'gx')
- pressure: float32 [64, 1024, 1024], P('gy', 'gx')
- residual: float32 [64, 1024, 1024], P('gy', 'gx')
Inputs may be any that keep to these rules, and one draw needn't show every extreme that they name: Row 0 of well_cells gives each well's layer, below 64; rows 1 and 2 its cell along the second and third dimensions, below 1024 and 1024. Wells may share a cell; their rates then add.
All inputs are finite; a program needn't handle non-finite values.
Results may differ from a plain program's by a relative error of at most 0.00024.
Values sent between devices are 32-bit elements; how exact they have to be, the bound alone decides.
No kernel may reach another device: no remote copies, remote signals or barrier semaphores. Data moves between devices by JAX's collectives and lax.ppermute only.
A program may use at most 128 MiB of HBM per device.

v0:
```python
import math

import jax
import jax.numpy as jnp
import numpy as np
from jax import lax
from jax.experimental import pallas as pl
from jax.experimental.pallas import tpu as pltpu
from jax.sharding import PartitionSpec as P


AMPLITUDE = 4.0
BF16 = jnp.bfloat16
F32 = jnp.float32
INTERPRET = False
HALO = 4


def call(body, outs, *args, specs=None, scratch=(), limit=60):
    return pl.pallas_call(
        body,
        out_shape=outs,
        in_specs=specs or [pl.BlockSpec(memory_space=pltpu.VMEM)] * len(args),
        scratch_shapes=scratch,
        interpret=INTERPRET,
        compiler_params=pltpu.CompilerParams(vmem_limit_bytes=limit * 2**20),
    )(*args)


def f32(*shape):
    return jax.ShapeDtypeStruct(shape, F32)


def on_chip(array):
    return array if INTERPRET else pltpu.with_memory_space_constraint(array, pltpu.MemorySpace.VMEM)


def halves(table):
    high = table.astype(BF16)
    low = (table - high.astype(np.float64)).astype(BF16)
    return jnp.asarray(high), jnp.asarray(low)


def cosine_sine(product, length):
    angle = (product % length).astype(np.float64) * (2.0 * math.pi / length)
    return np.cos(angle), np.sin(angle)


def table_y(length):
    half = length // 2
    k = np.arange(half).reshape(half // 2, 2).T
    cos, sin = cosine_sine(k[:, :, None] * np.arange(half), length)
    return np.stack([cos, -sin], axis=1).reshape(2 * half, half)


def tables_zx(gx, gy, zl, xl):
    row_x, row_z = np.repeat(np.arange(gx), gy), np.tile(np.arange(gy), gx)
    col_x, col_z = np.tile(np.arange(xl), zl), np.repeat(np.arange(zl), xl)

    def table(left_x, right_x, left_z, right_z, size_x, size_z):
        phase = np.outer(left_x, right_x) / size_x + np.outer(left_z, right_z) / size_z
        return np.exp(-2j * math.pi * phase)

    outer = table(row_x, row_x, row_z, row_z, gx, gy)
    twiddle = table(row_x, col_x, row_z, col_z, gx * xl, gy * zl)
    inner = table(col_x, col_x, col_z, col_z, xl, zl)
    forward = np.block([[inner.real, inner.imag], [-inner.imag, inner.real]])
    return outer, twiddle, forward


def tables_back(gx, gh, zl, xl):
    row_x, row_z = np.repeat(np.arange(gx), gh), np.tile(np.arange(gh), gx)
    layers = 2 * zl
    col_x, col_z = np.tile(np.arange(xl), layers), np.repeat(np.arange(layers), xl)
    edge = np.concatenate([np.arange(HALO), np.arange(xl - HALO, xl)])
    pick = (np.arange(layers)[:, None] * xl + edge).reshape(-1)
    freq_x = np.tile(np.arange(xl), layers)
    freq_z = np.repeat((np.arange(2)[:, None] + 2 * np.arange(zl)[None, :]).reshape(-1), xl)

    def table(left_x, right_x, left_z, right_z, size_x, size_z):
        phase = np.outer(left_x, right_x) / size_x + np.outer(left_z, right_z) / size_z
        return np.exp(2j * math.pi * phase)

    inner = table(freq_x, col_x, freq_z, col_z, xl, layers)
    twiddle = table(row_x, col_x, row_z, col_z, gx * xl, gh * layers)
    outer = table(row_x, row_x, row_z, row_z, gx, gh)
    blocks = [np.block([[t.real, t.imag], [-t.imag, t.real]]) for t in (inner, inner[:, pick])]
    edge_twiddle = twiddle[:, pick]
    edge_a = np.concatenate([edge_twiddle.real, edge_twiddle.real], axis=1)
    edge_b = np.concatenate([-edge_twiddle.imag, edge_twiddle.imag], axis=1)
    plain = [jnp.asarray(t, F32) for t in (twiddle.real, twiddle.imag, edge_a, edge_b)]
    return [*halves(np.concatenate(blocks, axis=1)), *plain, *halves(outer.real), *halves(outer.imag)]


def split(data):
    high = data.astype(BF16)
    return high, (data - high.astype(F32)).astype(BF16)


def dot(a, b):
    return jnp.dot(a, b, preferred_element_type=F32)


def left_product(table, data):
    (th, tl), (dh, dl) = table, data
    return dot(th, dh) + (dot(th, dl) + dot(tl, dh))


def right_product(data, table):
    (dh, dl), (th, tl) = data, table
    return dot(dh, th) + (dot(dl, th) + dot(dh, tl))


def mix_bits(seed_rows, cells):
    shift = lax.shift_right_logical
    hashed = seed_rows + cells * jnp.int32(-1640531535)
    hashed = hashed ^ shift(hashed, jnp.int32(16))
    hashed = hashed * jnp.int32(-2048144789)
    hashed = hashed ^ shift(hashed, jnp.int32(13))
    hashed = hashed * jnp.int32(-1028477387)
    hashed = hashed ^ shift(hashed, jnp.int32(16))
    value = shift(hashed, jnp.int32(8)).astype(F32)
    return (value + 0.5) * (2.0 * math.sqrt(3.0) / 16777216.0) - math.sqrt(3.0)


def noise_kernel(seed_ref, th_ref, tl_ref, out_ref):
    rows, half = th_ref.shape
    seeds = jnp.concatenate([seed_ref[layer : layer + 1] for layer in range(seed_ref.shape[0])], axis=1)
    cells = lax.broadcasted_iota(jnp.int32, (half, seeds.shape[1]), 0)
    near = mix_bits(seeds, cells)
    far = mix_bits(seeds, cells + half)
    mid, count = rows // 2, half // 2
    for parity, data in enumerate((near + far, near - far)):
        at = slice(parity * mid, (parity + 1) * mid)
        product = left_product((th_ref[at], tl_ref[at]), split(data))
        out_ref[pl.ds(2 * parity, count, stride=4), :] = product[:count]
        out_ref[pl.ds(2 * parity + 1, count, stride=4), :] = product[count:]


def power(base, exponent):
    return jnp.exp(exponent * jnp.log(base))


def spectrum_kernel(sizes, device_ref, lengths_ref, exponents_ref, data_ref, ar_h, ar_l, ai_h, ai_l, tr_ref, ti_ref, fh_ref, fl_ref, bh_ref, bl_ref, br_ref, bi_ref, ea_ref, eb_ref, or_h, or_l, oi_h, oi_l, *rest):
    out_ref = rest[-1]
    gx, gy, zl, xl, length_y = sizes
    rows, cols = gx * gy, zl * xl
    outer_r = (ar_h[...], ar_l[...])
    outer_i = (ai_h[...], ai_l[...])
    tr, ti = tr_ref[...], ti_ref[...]
    shape = (rows, cols)
    row = lax.broadcasted_iota(jnp.int32, shape, 0)
    col = lax.broadcasted_iota(jnp.int32, shape, 1)
    kx = lax.div(row, gy) + gx * lax.rem(col, xl)
    kz = lax.rem(row, gy) + gy * lax.div(col, xl)
    ky = device_ref[0]

    def wave(index, length):
        folded = jnp.minimum(index, length - index)
        return folded.astype(F32) * (2.0 * math.pi / length)

    ky_all = jnp.full((8, cols), ky, jnp.int32)
    total_y = 1.0 + power(lengths_ref[2] * wave(ky_all, length_y), exponents_ref[2])
    weight = jnp.where(ky_all == 0, 1.0, 2.0)
    volume = jnp.full((8, cols), lengths_ref[0] * lengths_ref[1] * lengths_ref[2], F32)
    scale = 1.0 / (gx * xl * gy * zl * length_y)
    numerator = AMPLITUDE * jnp.sqrt(volume) * scale * weight
    total = power(lengths_ref[0] * wave(kz, gy * zl), exponents_ref[0])
    total = total + power(lengths_ref[1] * wave(kx, gx * xl), exponents_ref[1])
    gain = numerator[:1] / (total_y[:1] + total)
    data = jnp.concatenate([data_ref[pl.ds(0, rows, stride=2), :], data_ref[pl.ds(1, rows, stride=2), :]], axis=1)
    parts = split(data)
    pr, pi = left_product(outer_r, parts), left_product(outer_i, parts)
    yr, yi = pr[:, :cols] - pi[:, cols:], pr[:, cols:] + pi[:, :cols]
    data = jnp.concatenate([yr * tr - yi * ti, yr * ti + yi * tr], axis=1)
    data = right_product(split(data), (fh_ref[...], fl_ref[...]))
    data = data * jnp.concatenate([gain, gain], axis=1)
    chips = gy // 2
    count, wide = gx * chips, 2 * cols
    data = data.reshape(gx, gy, wide)
    low = data[:, :chips].reshape(count, wide)
    high = data[:, chips:].reshape(count, wide)
    data = jnp.concatenate([low[:, :cols], high[:, :cols], low[:, cols:], high[:, cols:]], axis=1)
    data = right_product(split(data), (bh_ref[...], bl_ref[...]))
    yr, yi, edge = data[:, :wide], data[:, wide : 2 * wide], data[:, 2 * wide :]
    tr, ti = br_ref[...], bi_ref[...]
    turn = edge.shape[1] // 2
    edge = edge * ea_ref[...] + pltpu.roll(edge, turn, 1) * eb_ref[...]
    parts = split(jnp.concatenate([yr * tr - yi * ti, yr * ti + yi * tr, edge], axis=1))
    pr = left_product((or_h[...], or_l[...]), parts)
    pi = left_product((oi_h[...], oi_l[...]), parts)
    lane = lax.broadcasted_iota(jnp.int32, edge.shape, 1)
    turned = pltpu.roll(pi[:, 2 * wide :], turn, 1)
    edge = pr[:, 2 * wide :] + jnp.where(lane < turn, -turned, turned)
    edge = jnp.where(lax.rem(lane, 2 * HALO) < HALO, pltpu.roll(edge, count - chips, 0), pltpu.roll(edge, chips, 0))
    out = jnp.concatenate([pr[:, :wide] - pi[:, wide : 2 * wide], pr[:, wide : 2 * wide] + pi[:, :wide], edge], axis=1)
    pieces = out.shape[1] // 128
    for piece in range(pieces):
        out_ref[pl.ds(piece, count, stride=pieces), :] = out[:, piece * 128 : (piece + 1) * 128]


def edge_rows(value, xl, low_ref, high_ref, base):
    for layer in range(value.shape[0] // xl):
        at = base + layer * HALO
        low_ref[at : at + HALO] = value[layer * xl : layer * xl + HALO]
        high_ref[at : at + HALO] = value[(layer + 1) * xl - HALO : (layer + 1) * xl]


def widen(value_ref, low_ref, high_ref, base, xl, out_ref):
    for layer in range(value_ref.shape[0] // xl):
        to, at = layer * (xl + 2 * HALO), base + layer * HALO
        out_ref[to : to + xl] = value_ref[layer * xl : (layer + 1) * xl]
        out_ref[to + xl : to + xl + HALO] = high_ref[at : at + HALO]
        out_ref[to + xl + HALO : to + xl + 2 * HALO] = low_ref[at : at + HALO]


def field_kernel(xl, device_ref, data_ref, th_ref, tl_ref, *refs):
    both_ref, own_ref, other_ref = refs[-3:]
    rows, half = th_ref.shape
    mid, count = rows // 2, half // 2
    pieces = data_ref.shape[0] // count
    data = jnp.concatenate([data_ref[pl.ds(piece, count, stride=pieces), :] for piece in range(pieces)], axis=1)
    turned = jnp.transpose(data)
    wide = (turned.shape[0] - 128) // 2
    edge = turned[2 * wide :]
    left = jnp.concatenate([turned[:wide], turned[wide : 2 * wide]], axis=1)
    edge = jnp.concatenate([edge[:64], edge[64:]], axis=1)
    core = lax.rem(device_ref[0], 2)
    at = pl.ds(pl.multiple_of(core * mid, mid), mid)
    part = right_product(split(jnp.concatenate([left, edge], axis=0)), (th_ref[at, :], tl_ref[at, :]))
    layers = wide // xl // 2
    sums = []
    for side in range(2):
        found = []
        for layer in range(side * layers, (side + 1) * layers):
            found.append(part[layer * xl : (layer + 1) * xl])
            found.append(part[wide + layer * 2 * HALO : wide + (layer + 1) * 2 * HALO])
        sums.append(jnp.concatenate(found, axis=0))
    own = jnp.where(core == 0, sums[0], sums[1])
    other = jnp.where(core == 0, sums[1], sums[0])
    size = own.shape[0]
    own_ref[...] = own
    other_ref[...] = other
    both_ref[:size] = own
    both_ref[size:] = other


def rhs_kernel(xl, gy, device_ref, recharge_ref, cells_ref, rates_ref, storage_ref, rhs_ref, low_ref, high_ref):
    rows, length = recharge_ref.shape
    wells = cells_ref.shape[1]
    at_x, at_y = lax.div(device_ref[0], gy), lax.rem(device_ref[0], gy)
    layer = cells_ref[0:1] - at_y * (rows // xl)
    line = cells_ref[1:2] - at_x * xl
    inside = (line >= 0) & (line < xl)
    at = jnp.where(inside, layer * xl + line, -1)
    rate = jnp.where(lax.broadcasted_iota(jnp.int32, (rows, wells), 0) == at, rates_ref[...], 0.0)
    column = (lax.broadcasted_iota(jnp.int32, (length, wells), 0) == cells_ref[2:3]).astype(F32).astype(BF16)
    added = None
    for _ in range(3):
        part = rate.astype(BF16)
        rate = rate - part.astype(F32)
        product = lax.dot_general(part, column, (((1,), (1,)), ((), ())), preferred_element_type=F32)
        added = product if added is None else added + product
    rhs = recharge_ref[...] + added
    rhs_ref[...] = rhs
    edge_rows(storage_ref[...], xl, low_ref, high_ref, 0)
    edge_rows(rhs, xl, low_ref, high_ref, rows // xl * HALO)


def widen_pair_kernel(xl, storage_ref, rhs_ref, low_ref, high_ref, s_ref, r_ref, first_ref, last_ref):
    layers, wide = storage_ref.shape[0] // xl, xl + 2 * HALO
    widen(storage_ref, low_ref, high_ref, 0, xl, s_ref)
    widen(rhs_ref, low_ref, high_ref, layers * HALO, xl, r_ref)
    size = (layers - 1) * wide
    first_ref[:size] = s_ref[:size]
    first_ref[size:] = r_ref[:size]
    last_ref[:size] = s_ref[wide:]
    last_ref[size:] = r_ref[wide:]


def krylov_kernel(xl, gx, gy, device_ref, both_ref, swap_ref, far_a, far_b, s_ref, r_ref, sr_low, sr_high, log_ref, u0_out, u1_out, u2_out, u3_out, diag_out, mom_out, q_all, cz, cx, cy, inv, u0, u1, u2, u3, diag):
    wide, length = xl + 2 * HALO, s_ref.shape[1]
    own = s_ref.shape[0] // wide
    total = own + 2 * HALO
    at_x, at_y = lax.div(device_ref[0], gy), lax.rem(device_ref[0], gy)
    sides = (at_y > 0, at_y < gy - 1, at_x > 0, at_x < gx - 1)
    z_lo, z_hi, x_lo, x_hi = (jnp.where(side, 1.0, 0.0) for side in sides)
    row = lax.broadcasted_iota(jnp.int32, (wide, length), 0)
    lane = lax.broadcasted_iota(jnp.int32, (wide, length), 1)
    keep_x = jnp.where(row == xl - 1, x_hi, jnp.where(row == wide - 1, x_lo, 1.0))
    keep_y = jnp.where(lane == length - 1, 0.0, 1.0)

    def at(z):
        return pl.ds(z * wide, wide)

    core = lax.rem(device_ref[0], 2)
    sign = jnp.where(core == 0, 1.0, -1.0)
    size, half = own * wide, length // 2
    first, second = slice(0, size), slice(size, 2 * size)
    full = slice(0, size)
    near = jnp.where(core == 0, 2 * size, 0)
    groups = (
        (both_ref, first, swap_ref, second, size),
        (both_ref, second, swap_ref, first, near),
        (far_a, full, far_b, full, 2 * size - near),
    )
    for group, (a_ref, a_at, b_ref, b_at, start) in enumerate(groups):
        to = pl.ds(pl.multiple_of(start, 8), size)
        a, b = a_ref[a_at], b_ref[b_at]
        lower, upper = a + b, (a - b) * sign
        q_all[to, :half] = 0.5 * jnp.exp(-lower)
        q_all[to, half:] = 0.5 * jnp.exp(-upper)
        if group == 0:
            for layer in range(own):
                log_ref[layer * xl : (layer + 1) * xl, :half] = lower[layer * wide : layer * wide + xl]
                log_ref[layer * xl : (layer + 1) * xl, half:] = upper[layer * wide : layer * wide + xl]

    def q_of(z):
        return q_all[at(z)]

    def pair_of(z):
        depth = own - 1
        if z < HALO:
            return sr_low[at(z - 1)], sr_low[at(depth + z - 1)]
        if z >= HALO + own:
            return sr_high[at(z - HALO - own)], sr_high[at(depth + z - HALO - own)]
        return s_ref[at(z - HALO)], r_ref[at(z - HALO)]

    def up_x(value):
        return pltpu.roll(value, wide - 1, 0)

    def down_x(value):
        return pltpu.roll(value, 1, 0)

    def up_y(value):
        return pltpu.roll(value, length - 1, 1)

    def down_y(value):
        return pltpu.roll(value, 1, 1)

    for z in range(total - 1):
        face = pl.reciprocal(q_of(z) + q_of(z + 1))
        if z == HALO - 1:
            face = face * z_lo
        if z == HALO + own - 1:
            face = face * z_hi
        cz[at(z)] = face
        if z == 0:
            continue
        q = q_of(z)
        storage, rhs = pair_of(z)
        face_x = pl.reciprocal(q + up_x(q)) * keep_x
        face_y = pl.reciprocal(q + up_y(q)) * keep_y
        cx[at(z)] = face_x
        cy[at(z)] = face_y
        d = storage + cz[at(z - 1)] + face + face_x + down_x(face_x) + face_y + down_y(face_y)
        inverse = pl.reciprocal(d)
        inv[at(z)] = inverse
        u0[at(z)] = rhs * inverse
        if HALO <= z < HALO + own:
            diag[pl.ds((z - HALO) * xl, xl)] = d[:xl]
    levels = (u0, u1, u2, u3)
    for level in range(3):
        old, new = levels[level], levels[level + 1]
        for z in range(2 + level, total - 2 - level):
            here, face_x, face_y = old[at(z)], cx[at(z)], cy[at(z)]
            flow = cz[at(z - 1)] * old[at(z - 1)] + cz[at(z)] * old[at(z + 1)]
            flow = flow + face_x * up_x(here) + down_x(face_x * here)
            flow = flow + face_y * up_y(here) + down_y(face_y * here)
            new[at(z)] = flow * inv[at(z)]
    sums = [None] * 6
    for z in range(HALO, HALO + own):
        to = pl.ds((z - HALO) * xl, xl)
        d = diag[to]
        values = [level[pl.ds(z * wide, xl)] for level in levels]
        for out, value in zip((u0_out, u1_out, u2_out, u3_out), values):
            out[to] = value
        diag_out[to] = d
        for i in range(6):
            if i % 2 == 0:
                weighted = d * values[i // 2]
            term = weighted * values[(i + 1) // 2]
            term = jnp.sum(term, axis=0, keepdims=True)
            sums[i] = term if sums[i] is None else sums[i] + term
    place = lax.broadcasted_iota(jnp.int32, (1, 128), 1)
    moments = jnp.zeros((1, 128), F32)
    for i in range(6):
        moments = jnp.where(place == i, jnp.sum(sums[i], axis=1, keepdims=True), moments)
    mom_out[...] = jnp.broadcast_to(moments, mom_out.shape)


def partial_kernel(in_ref, out_ref):
    out_ref[...] = jnp.broadcast_to(jnp.sum(in_ref[...], axis=0, keepdims=True), out_ref.shape)


def final_kernel(iters, mom_ref, u0, u1, u2, u3, diag_ref, pressure_ref, residual_ref):
    moments = jnp.sum(mom_ref[...], axis=0, keepdims=True)
    lane = lax.broadcasted_iota(jnp.int32, (1, 128), 1)
    nu = [jnp.sum(jnp.where(lane == i, moments, 0.0), axis=1, keepdims=True) for i in range(2 * iters)]

    def form(a, b):
        total = None
        for i, left in enumerate(a):
            for j, right in enumerate(b):
                term = left * right * nu[i + j]
                total = term if total is None else total + term
        return total

    one = jnp.ones((1, 1), F32)
    zero = jnp.zeros((1, 1), F32)
    precond, direction, pressure = [one], [one], [zero] * iters
    rz = nu[0]
    for it in range(iters):
        image = [
            (direction[i] if i < len(direction) else zero) - (direction[i - 1] if i > 0 else zero)
            for i in range(len(direction) + 1)
        ]
        alpha = rz / form(direction, image)
        pressure = [old + alpha * direction[i] if i < len(direction) else old for i, old in enumerate(pressure)]
        precond = [(precond[i] if i < len(precond) else zero) - alpha * image[i] for i in range(len(image))]
        if it + 1 < iters:
            new = form(precond, precond)
            beta = new / rz
            direction = [
                precond[i] + beta * direction[i] if i < len(direction) else precond[i] for i in range(len(precond))
            ]
            rz = new
    basis = [u0[...], u1[...], u2[...], u3[...]]
    pressure_ref[...] = pressure[0] * basis[0] + pressure[1] * basis[1] + pressure[2] * basis[2]
    total = precond[0] * basis[0] + precond[1] * basis[1] + precond[2] * basis[2] + precond[3] * basis[3]
    residual_ref[...] = diag_ref[...] * total


ITERS = 3


def exchange(low, high, axis):
    count = lax.axis_size(axis)
    up = [(i, i + 1) for i in range(count - 1)]
    down = [(i + 1, i) for i in range(count - 1)]
    from_low = lax.ppermute(high, axis, up)
    return from_low, lax.ppermute(low, axis, down)


def shards(seeds, lengths, exponents, storage, recharge, well_cells, well_rates):
    zl, xl, length_y = storage.shape
    gx, gh = lax.axis_size("gx"), lax.axis_size("gh")
    gy = 2 * gh
    assert zl == HALO and xl >= HALO
    rows, wide = zl * xl, xl + 2 * HALO
    block, middle, part = f32(rows, length_y), f32(zl * wide, length_y), f32(2 * (zl - 1) * wide, length_y)
    edge_pair = f32(2 * zl * HALO, length_y)
    at_x, at_y = lax.axis_index("gx"), lax.axis_index(("gh", "core"))
    device = (at_x * gy + at_y).reshape(1).astype(jnp.int32)
    smem = pl.BlockSpec(memory_space=pltpu.SMEM)
    vmem = pl.BlockSpec(memory_space=pltpu.VMEM)
    ty = halves(table_y(length_y))
    outer, twiddle, inner = tables_zx(gx, gy, zl, xl)
    tables = [*halves(outer.real), *halves(outer.imag), jnp.asarray(twiddle.real, F32), jnp.asarray(twiddle.imag, F32)]
    tables += [*halves(inner), *tables_back(gx, gh, zl, xl)]

    def everywhere(array, axes):
        return on_chip(lax.all_to_all(array, axes, split_axis=0, concat_axis=0, tiled=True).reshape(-1, array.shape[-1] if array.ndim == 2 else 128))

    flat_storage = storage.reshape(rows, length_y)
    rhs, low, high = call(
        lambda *refs: rhs_kernel(xl, gy, *refs),
        [block, edge_pair, edge_pair],
        device,
        recharge.reshape(rows, length_y),
        well_cells,
        well_rates.reshape(1, -1),
        flat_storage,
        specs=[smem] + [vmem] * 4,
    )
    pair_x = exchange(low, high, "gx")
    wide_storage, wide_rhs, first, last = call(
        lambda *refs: widen_pair_kernel(xl, *refs), [middle, middle, part, part], flat_storage, rhs, *pair_x
    )
    pair_low, pair_high = exchange(first, last, ("gh", "core"))

    spectrum = call(noise_kernel, f32(length_y, rows), seeds, *ty)
    spectrum = everywhere(spectrum, ("gx", "gh", "core"))
    chips, message = gx * gh, 4 * rows + 128
    spectrum = call(
        lambda *refs: spectrum_kernel((gx, gy, zl, xl, length_y), *refs),
        f32(chips * message // 128, 128),
        device,
        lengths,
        exponents,
        spectrum,
        *tables,
        specs=[smem, smem, smem] + [vmem] * (1 + len(tables)),
    )
    spectrum = everywhere(spectrum.reshape(chips, 1, message), ("gx", "gh"))
    partial = f32(zl * wide, length_y // 2)
    both, own, other = call(
        lambda *refs: field_kernel(xl, *refs),
        [f32(2 * zl * wide, length_y // 2), partial, partial],
        device,
        spectrum,
        *ty,
        first,
        specs=[smem] + [vmem] * 3 + [pl.BlockSpec(memory_space=pl.ANY)],
    )
    far = [(2 * c, 2 * c + 2) for c in range(gh - 1)] + [(2 * c + 3, 2 * c + 1) for c in range(gh - 1)]
    beside = [(2 * c + 1, 2 * c + 2) for c in range(gh - 1)] + [(2 * c + 2, 2 * c + 1) for c in range(gh - 1)]
    far_a = on_chip(lax.ppermute(other, ("gh", "core"), far))
    far_b = on_chip(lax.ppermute(own, ("gh", "core"), beside))
    swap = on_chip(lax.ppermute(both, "core", [(0, 1), (1, 0)]))

    layers = zl + 2 * HALO
    log_perm, *basis, diag, moments = call(
        lambda *refs: krylov_kernel(xl, gx, gy, *refs),
        [block] * 6 + [f32(gx, 128)],
        device,
        both,
        swap,
        far_a,
        far_b,
        wide_storage,
        wide_rhs,
        pair_low,
        pair_high,
        specs=[smem] + [vmem] * 8,
        scratch=[pltpu.VMEM((layers * wide, length_y), F32)] * 9 + [pltpu.VMEM((rows, length_y), F32)],
        limit=60,
    )
    moments = lax.all_to_all(moments, "gx", split_axis=0, concat_axis=0, tiled=True)
    moments = call(partial_kernel, f32(gy, 128), moments)
    moments = lax.all_to_all(moments, ("gh", "core"), split_axis=0, concat_axis=0, tiled=True)
    pressure, residual = call(
        lambda *refs: final_kernel(ITERS, *refs), [block, block], moments, *basis, diag
    )
    shape = storage.shape
    return (log_perm.reshape(shape), pressure.reshape(shape), residual.reshape(shape))


def solution(mesh):
    gx, gy = mesh.devices.shape
    mesh = jax.sharding.Mesh(mesh.devices.reshape(gx, gy // 2, 2), ("gx", "gh", "core"))
    z = ("gh", "core")
    block = P(z, "gx", None)
    placed = (P(z, "gx"), P(), P(), block, block, P(), P())

    return jax.shard_map(shards, mesh=mesh, in_specs=placed, out_specs=(block, block, block), check_vma=False)
```

profile of v0, /device:TPU:1, one launch (start us, length us, event | category | flops | bytes accessed | tf_op | source)
XLA Modules:
  0.0 155.8 jit_solution(14189763299444422063)
XLA Ops:
  0.6 3.6 %shard_map.274 = f32[1024,128]{1,0:T(8,128)} custom-call(s32[4,32]{1,0:T(4,128)} %seed_ref.1, bf16[1024,512]{1,0:T(8,128)(2,1)} %constant.58.clone.th_ref.refs_2_, bf16[1024,512]{1,0:T(8,128)(2,1)} %constant.59.clone.tl_ref.refs_3_), custom_call_target="tpu_custom_call" | custom-call | tf_op jit(solution)/shard_map/pallas_call | solution.py:20
  4.2 22.1 %all-to-all-start = ((f32[512,2,128]{2,1,0:T(2,128)}), f32[512,2,128]{2,1,0:T(2,128)S(1)}, u32[]{:S(2)}, u32[]{:S(2)}) async-start(f32[512,2,128]{2,1,0:T(2,128)} %bitcast.24), calls=%async_computation | async-start | bytes 1048576 | tf_op jit(solution)/shard_map/all_to_all | solution.py:463
  26.4 21.9 %all-to-all-done = f32[512,2,128]{2,1,0:T(2,128)S(1)} async-done(((f32[512,2,128]{2,1,0:T(2,128)}), f32[512,2,128]{2,1,0:T(2,128)S(1)}, u32[]{:S(2)}, u32[]{:S(2)}) %all-to-all-start) | async-done | bytes 524320 | tf_op jit(solution)/shard_map/all_to_all | solution.py:463
  48.3 6.8 %shard_map.275 = f32[1280,128]{1,0:T(8,128)} custom-call(s32[1]{0:T(128)} %bitcast.refs_0_, f32[3]{0:T(128)} %refs_1_.1, f32[3]{0:T(128)} %refs_2_.3, f32[1024,128]{1,0:T(8,128)S(1)} %bitcast.20, bf16[512,512]{1,0:T(8,128)(2,1)} %constant.60.clone.refs_4_, bf16[512,512]{1,0:T(8,128)(2,1)} %constant.61.clone.refs_5_, ...), custom_call_target="tpu_custom_call" | custom-call | tf_op jit(solution)/shard_map/pallas_call | solution.py:20
  55.1 9.8 %all-to-all-start.1 = ((f32[256,1,640]{2,1,0:T(1,128)}), f32[256,1,640]{2,1,0:T(1,128)S(1)}, u32[]{:S(2)}, u32[]{:S(2)}) async-start(f32[256,1,640]{2,1,0:T(1,128)} %bitcast.21), calls=%async_computation.1 | async-start | bytes 1310720 | tf_op jit(solution)/shard_map/all_to_all | solution.py:463
  64.9 2.8 %shard_map.276 = (f32[128,1024]{1,0:T(8,128)}, f32[32,1024]{1,0:T(8,128)}, f32[32,1024]{1,0:T(8,128)}) custom-call(s32[1]{0:T(128)} %bitcast.refs_0_, f32[128,1024]{1,0:T(8,128)} %bitcast.25, s32[3,256]{1,0:T(4,128)} %refs_2_.4, f32[1,256]{1,0:T(1,128)} %bitcast.30, f32[128,1024]{1,0:T(8,128)} %bitcast.22), custom_call_target="tpu_custom_call" | custom-call | tf_op jit(solution)/shard_map/pallas_call | solution.py:20
  67.7 1.6 %collective-permute-start = (f32[32,1024]{1,0:T(8,128)}, f32[32,1024]{1,0:T(8,128)S(1)}, u32[]{:S(2)}, u32[]{:S(2)}) collective-permute-start(f32[32,1024]{1,0:T(8,128)} %get-tuple-element.23), channel_id=1, source_target_pairs={{0,16},{16,32},{32,48},{48,64},{64,80},{80,96},{96,112},{112,128},... | collective-permute-start | bytes 393224 | tf_op jit(solution)/shard_map/ppermute | solution.py:441
  69.3 1.3 collective-permute-start.1
  70.6 9.7 %collective-permute-done.refs_2_ = f32[32,1024]{1,0:T(8,128)S(1)} collective-permute-done((f32[32,1024]{1,0:T(8,128)}, f32[32,1024]{1,0:T(8,128)S(1)}, u32[]{:S(2)}, u32[]{:S(2)}) %collective-permute-start) | collective-permute-done | bytes 131104 | tf_op jit(solution)/shard_map/ppermute | solution.py:441
  80.2 2.2 %collective-permute-done.1.refs_3_ = f32[32,1024]{1,0:T(8,128)S(1)} collective-permute-done((f32[32,1024]{1,0:T(8,128)}, f32[32,1024]{1,0:T(8,128)S(1)}, u32[]{:S(2)}, u32[]{:S(2)}) %collective-permute-start.1) | collective-permute-done | bytes 131104 | tf_op jit(solution)/shard_map/ppermute | solution.py:442
  83.0 3.0 %shard_map.277 = (f32[160,1024]{1,0:T(8,128)}, f32[160,1024]{1,0:T(8,128)}, f32[240,1024]{1,0:T(8,128)}, f32[240,1024]{1,0:T(8,128)}) custom-call(f32[128,1024]{1,0:T(8,128)} %bitcast.23, f32[128,1024]{1,0:T(8,128)} %get-tuple-element.22.refs_1_, f32[32,1024]{1,0:T(8,128)} %copy-done.2, f32[32,1024]{1,0:T(8,128)} %copy-done.3), custom_call_target="tpu_custom_call" | custom-call | tf_op jit(solution)/shard_map/pallas_call | solution.py:20
  86.1 3.0 %collective-permute-start.5 = (f32[240,1024]{1,0:T(8,128)}, f32[240,1024]{1,0:T(8,128)S(1)}, u32[]{:S(2)}, u32[]{:S(2)}) collective-permute-start(f32[240,1024]{1,0:T(8,128)} %get-tuple-element.31), channel_id=1, source_target_pairs={{0,1},{1,2},{2,3},{3,4},{4,5},{5,6},{6,7},{7,8},{8,9},{9,10},{10,1... | collective-permute-start | bytes 2949128 | tf_op jit(solution)/shard_map/ppermute | solution.py:441
  89.1 1.9 %collective-permute-start.6 = (f32[240,1024]{1,0:T(8,128)}, f32[240,1024]{1,0:T(8,128)S(1)}, u32[]{:S(2)}, u32[]{:S(2)}) collective-permute-start(f32[240,1024]{1,0:T(8,128)} %get-tuple-element.25.refs_4_), channel_id=1, source_target_pairs={{1,0},{2,1},{3,2},{4,3},{5,4},{6,5},{7,6},{8,7},{9,8},{10,9},{11,1... | collective-permute-start | bytes 2949128 | tf_op jit(solution)/shard_map/ppermute | solution.py:442
  91.0 3.4 %shard_map.278 = (f32[320,512]{1,0:T(8,128)}, f32[160,512]{1,0:T(8,128)}, f32[160,512]{1,0:T(8,128)}) custom-call(s32[1]{0:T(128)} %bitcast.refs_0_, f32[1280,128]{1,0:T(8,128)S(1)} %bitcast.19, bf16[1024,512]{1,0:T(8,128)(2,1)} %constant.58.clone.th_ref.refs_2_, bf16[1024,512]{1,0:T(8,128)(2,1)} %constant.59.clone.tl_ref.refs_3_, ...), custom_call_target="tpu_custom_call" | custom-call | tf_op jit(solution)/shard_map/pallas_call | solution.py:20
  94.4 1.9 %collective-permute-start.2 = (f32[320,512]{1,0:T(8,128)}, f32[320,512]{1,0:T(8,128)S(1)}, u32[]{:S(2)}, u32[]{:S(2)}) collective-permute-start(f32[320,512]{1,0:T(8,128)} %get-tuple-element.26.refs_1_), channel_id=1, source_target_pairs={{0,1},{1,0},{2,3},{3,2},{4,5},{5,4},{6,7},{7,6},{8,9},{9,8},{10,11... | collective-permute-start | bytes 1966088 | tf_op jit(solution)/shard_map/ppermute | solution.py:510
  96.4 1.3 collective-permute-start.3
  97.7 6.0 %collective-permute-start.4 = (f32[160,512]{1,0:T(8,128)}, f32[160,512]{1,0:T(8,128)S(1)}, u32[]{:S(2)}, u32[]{:S(2)}) collective-permute-start(f32[160,512]{1,0:T(8,128)} %get-tuple-element.28), channel_id=1, source_target_pairs={{1,2},{3,4},{5,6},{7,8},{9,10},{11,12},{13,14},{2,1},{4,3},{6,5},{... | collective-permute-start | bytes 983048 | tf_op jit(solution)/shard_map/ppermute | solution.py:509
  103.7 4.5 %collective-permute-done.6.refs_8_ = f32[240,1024]{1,0:T(8,128)S(1)} collective-permute-done((f32[240,1024]{1,0:T(8,128)}, f32[240,1024]{1,0:T(8,128)S(1)}, u32[]{:S(2)}, u32[]{:S(2)}) %collective-permute-start.6) | collective-permute-done | bytes 983072 | tf_op jit(solution)/shard_map/ppermute | solution.py:442
  108.3 3.5 %collective-permute-done.4.refs_4_ = f32[160,512]{1,0:T(8,128)S(1)} collective-permute-done((f32[160,512]{1,0:T(8,128)}, f32[160,512]{1,0:T(8,128)S(1)}, u32[]{:S(2)}, u32[]{:S(2)}) %collective-permute-start.4) | collective-permute-done | bytes 327712 | tf_op jit(solution)/shard_map/ppermute | solution.py:509
  111.8 7.1 %shard_map.279 = (f32[128,1024]{1,0:T(8,128)}, f32[128,1024]{1,0:T(8,128)}, f32[128,1024]{1,0:T(8,128)}, f32[128,1024]{1,0:T(8,128)}, f32[128,1024]{1,0:T(8,128)...) custom-call(s32[1]{0:T(128)} %bitcast.refs_0_, f32[320,512]{1,0:T(8,128)} %get-tuple-element.26.refs_1_, ...), custom_call_target="tpu_custom_call" | custom-call | tf_op jit(solution)/shard_map/pallas_call | solution.py:20
  118.9 17.9 %all_to_all.38 = f32[32,1,128]{2,1,0:T(1,128)} all-to-all(f32[32,1,128]{2,1,0:T(1,128)} %bitcast.29), channel_id=1, replica_groups=mesh['gx'=32,'gh'=8,'core'=2] {'gx'}, dimensions={0} | all-to-all | bytes 32768 | tf_op jit(solution)/shard_map/all_to_all | solution.py:529
  136.8 1.3 shard_map.280
  138.1 14.5 %all_to_all.39 = f32[16,1,128]{2,1,0:T(1,128)} all-to-all(f32[16,1,128]{2,1,0:T(1,128)} %bitcast.28), channel_id=1, replica_groups=mesh['gx'=32,'gh'=8,'core'=2] {'gh','core'}, dimensions={0} | all-to-all | bytes 16384 | tf_op jit(solution)/shard_map/all_to_all | solution.py:531
  152.6 3.1 %shard_map.281 = (f32[128,1024]{1,0:T(8,128)}, f32[128,1024]{1,0:T(8,128)}) custom-call(f32[16,128]{1,0:T(8,128)} %bitcast.27, f32[128,1024]{1,0:T(8,128)} %get-tuple-element.34.refs_1_, f32[128,1024]{1,0:T(8,128)} %get-tuple-element.35.refs_2_, f32[128,1024]{1,0:T(8,128)} %get-tuple-element.36.refs_3_, f32[128,1024]{1,0:T(8,128)} %get-tuple-element.37.refs_4_, ...), custom_call_target="tpu_custom_call" | custom-call | tf_op jit(solution)/shard_map/pallas_call | solution.py:20
  (12 shorter events, 0.7 us)
Async XLA Ops:
  4.2 44.1 %all-to-all-start = ((f32[512,2,128]{2,1,0:T(2,128)}), f32[512,2,128]{2,1,0:T(2,128)S(1)}, u32[]{:S(2)}, u32[]{:S(2)}) async-start(f32[512,2,128]{2,1,0:T(2,128)} %bitcast.24), calls=%async_computation | async-start | bytes 1048576 | tf_op jit(solution)/shard_map/all_to_all | solution.py:463
  55.1 35.9 %all-to-all-start.1 = ((f32[256,1,640]{2,1,0:T(1,128)}), f32[256,1,640]{2,1,0:T(1,128)S(1)}, u32[]{:S(2)}, u32[]{:S(2)}) async-start(f32[256,1,640]{2,1,0:T(1,128)} %bitcast.21), calls=%async_computation.1 | async-start | bytes 1310720 | tf_op jit(solution)/shard_map/all_to_all | solution.py:463
  67.7 12.6 %collective-permute-start = (f32[32,1024]{1,0:T(8,128)}, f32[32,1024]{1,0:T(8,128)S(1)}, u32[]{:S(2)}, u32[]{:S(2)}) collective-permute-start(f32[32,1024]{1,0:T(8,128)} %get-tuple-element.23), channel_id=1, source_target_pairs={{0,16},{16,32},{32,48},{48,64},{64,80},{80,96},{96,112},{112,128},... | collective-permute-start | bytes 393224 | tf_op jit(solution)/shard_map/ppermute | solution.py:441
  69.3 13.1 %collective-permute-start.1 = (f32[32,1024]{1,0:T(8,128)}, f32[32,1024]{1,0:T(8,128)S(1)}, u32[]{:S(2)}, u32[]{:S(2)}) collective-permute-start(f32[32,1024]{1,0:T(8,128)} %get-tuple-element.24), channel_id=1, source_target_pairs={{16,0},{32,16},{48,32},{64,48},{80,64},{96,80},{112,96},{128,112},... | collective-permute-start | bytes 393224 | tf_op jit(solution)/shard_map/ppermute | solution.py:442
  80.2 2.2 %copy-start.2 = (f32[32,1024]{1,0:T(8,128)}, f32[32,1024]{1,0:T(8,128)S(1)}, u32[]{:S(2)}) copy-start(f32[32,1024]{1,0:T(8,128)S(1)} %collective-permute-done.refs_2_) | copy-start | bytes 393220
  82.4 0.7 copy-start.3
  86.1 17.6 %collective-permute-start.5 = (f32[240,1024]{1,0:T(8,128)}, f32[240,1024]{1,0:T(8,128)S(1)}, u32[]{:S(2)}, u32[]{:S(2)}) collective-permute-start(f32[240,1024]{1,0:T(8,128)} %get-tuple-element.31), channel_id=1, source_target_pairs={{0,1},{1,2},{2,3},{3,4},{4,5},{5,6},{6,7},{7,8},{8,9},{9,10},{10,1... | collective-permute-start | bytes 2949128 | tf_op jit(solution)/shard_map/ppermute | solution.py:441
  89.1 19.1 %collective-permute-start.6 = (f32[240,1024]{1,0:T(8,128)}, f32[240,1024]{1,0:T(8,128)S(1)}, u32[]{:S(2)}, u32[]{:S(2)}) collective-permute-start(f32[240,1024]{1,0:T(8,128)} %get-tuple-element.25.refs_4_), channel_id=1, source_target_pairs={{1,0},{2,1},{3,2},{4,3},{5,4},{6,5},{7,6},{8,7},{9,8},{10,9},{11,1... | collective-permute-start | bytes 2949128 | tf_op jit(solution)/shard_map/ppermute | solution.py:442
  94.4 17.3 %collective-permute-start.2 = (f32[320,512]{1,0:T(8,128)}, f32[320,512]{1,0:T(8,128)S(1)}, u32[]{:S(2)}, u32[]{:S(2)}) collective-permute-start(f32[320,512]{1,0:T(8,128)} %get-tuple-element.26.refs_1_), channel_id=1, source_target_pairs={{0,1},{1,0},{2,3},{3,2},{4,5},{5,4},{6,7},{7,6},{8,9},{9,8},{10,11... | collective-permute-start | bytes 1966088 | tf_op jit(solution)/shard_map/ppermute | solution.py:510
  96.4 11.9 %collective-permute-start.3 = (f32[160,512]{1,0:T(8,128)}, f32[160,512]{1,0:T(8,128)S(1)}, u32[]{:S(2)}, u32[]{:S(2)}) collective-permute-start(f32[160,512]{1,0:T(8,128)} %get-tuple-element.27), channel_id=1, source_target_pairs={{0,2},{2,4},{4,6},{6,8},{8,10},{10,12},{12,14},{3,1},{5,3},{7,5},{... | collective-permute-start | bytes 983048 | tf_op jit(solution)/shard_map/ppermute | solution.py:508
  97.7 14.1 %collective-permute-start.4 = (f32[160,512]{1,0:T(8,128)}, f32[160,512]{1,0:T(8,128)S(1)}, u32[]{:S(2)}, u32[]{:S(2)}) collective-permute-start(f32[160,512]{1,0:T(8,128)} %get-tuple-element.28), channel_id=1, source_target_pairs={{1,2},{3,4},{5,6},{7,8},{9,10},{11,12},{13,14},{2,1},{4,3},{6,5},{... | collective-permute-start | bytes 983048 | tf_op jit(solution)/shard_map/ppermute | solution.py:509
  103.7 8.1 %copy-start = (f32[240,1024]{1,0:T(8,128)}, f32[240,1024]{1,0:T(8,128)S(1)}, u32[]{:S(2)}) copy-start(f32[240,1024]{1,0:T(8,128)S(1)} %collective-permute-done.5.refs_7_) | copy-start | bytes 2949124
  108.2 3.6 %copy-start.1 = (f32[240,1024]{1,0:T(8,128)}, f32[240,1024]{1,0:T(8,128)S(1)}, u32[]{:S(2)}) copy-start(f32[240,1024]{1,0:T(8,128)S(1)} %collective-permute-done.6.refs_8_) | copy-start | bytes 2949124
where the time goes:
time: 156 us
  starting transfers between devices  49 us (31%)
  waiting for transfers between devices  41.8 us (27%)
  blocking collectives  32.4 us (21%)
  Pallas kernels  31.1 us (20%)
    all_to_all x2, starting transfers between devices, everywhere(): lax.all_to_all(array, axes, split_axis=0, concat_axis=0, tiled=True)  31.9 us
    pallas_call x8, Pallas kernels, call(): pl.pallas_call(body, out_shape=outs, in_specs=specs or [pl.BlockSpec(memo...  31.1 us
    all_to_all x2, waiting for transfers between devices, everywhere(): lax.all_to_all(array, axes, split_axis=0, concat_axis=0, tiled=True)  21.9 us
    all_to_all x1, blocking collectives, shards(): lax.all_to_all(moments, 'gx', split_axis=0, concat_axis=0, tiled=True)  17.9 us
    all_to_all x1, blocking collectives, shards(): lax.all_to_all(moments, ('gh', 'core'), split_axis=0, concat_axis=0, tile...  14.5 us
    ppermute x2, waiting for transfers between devices, exchange(): from_low = lax.ppermute(high, axis, up)  9.65 us
    ppermute x2, waiting for transfers between devices, exchange(): return (from_low, lax.ppermute(low, axis, down))  6.67 us
    ppermute x1, starting transfers between devices, shards(): far_b = on_chip(lax.ppermute(own, ('gh', 'core'), beside))  6.01 us
  transfers between devices with their start and end apart: 9, of which 6 were waited for; matrix products, arithmetic and copies ran while one was open for 0% of the time, Pallas kernels for 6%

commit v1 on v0

--- a/solution.py
+++ b/solution.py
@@ -524,13 +524,13 @@
         pair_high,
         specs=[smem] + [vmem] * 8,
         scratch=[pltpu.VMEM((layers * wide, length_y), F32)] * 9 + [pltpu.VMEM((rows, length_y), F32)],
-        limit=60,
+        limit=44,
     )
     moments = lax.all_to_all(moments, "gx", split_axis=0, concat_axis=0, tiled=True)
-    moments = call(partial_kernel, f32(gy, 128), moments)
+    moments = call(partial_kernel, f32(gy, 128), moments, limit=4)
     moments = lax.all_to_all(moments, ("gh", "core"), split_axis=0, concat_axis=0, tiled=True)
     pressure, residual = call(
-        lambda *refs: final_kernel(ITERS, *refs), [block, block], moments, *basis, diag
+        lambda *refs: final_kernel(ITERS, *refs), [block, block], moments, *map(on_chip, (*basis, diag)), limit=16
     )
     shape = storage.shape
     return (log_perm.reshape(shape), pressure.reshape(shape), residual.reshape(shape))

time: 156 us -> 153 us (0.981)
  Pallas kernels: 31.1 us -> 26.5 us
    pallas_call x8, Pallas kernels: 31.1 us -> 26.5 us  [call(): pl.pallas_call(body, out_shape=outs, in_specs=specs or [pl.BlockSpec(memo...]
where the time goes in v1:
time: 153 us; the launch traced here: 152 us
  starting transfers between devices  49 us (32%)
  waiting for transfers between devices  41.7 us (27%)
  blocking collectives  32.4 us (21%)
  Pallas kernels  26.5 us (17%)
  local copies, waits for them, and re-layouts  1.74 us (1%)
    all_to_all x2, starting transfers between devices, everywhere(): lax.all_to_all(array, axes, split_axis=0, concat_axis=0, tiled=True)  31.9 us
    pallas_call x8, Pallas kernels, call(): pl.pallas_call(body, out_shape=outs, in_specs=specs or [pl.BlockSpec(memo...  26.5 us
    all_to_all x2, waiting for transfers between devices, everywhere(): lax.all_to_all(array, axes, split_axis=0, concat_axis=0, tiled=True)  21.9 us
    all_to_all x1, blocking collectives, shards(): lax.all_to_all(moments, 'gx', split_axis=0, concat_axis=0, tiled=True)  17.7 us
    all_to_all x1, blocking collectives, shards(): lax.all_to_all(moments, ('gh', 'core'), split_axis=0, concat_axis=0, tile...  14.7 us
    ppermute x2, waiting for transfers between devices, exchange(): from_low = lax.ppermute(high, axis, up)  9.75 us
    ppermute x2, waiting for transfers between devices, exchange(): return (from_low, lax.ppermute(low, axis, down))  6.35 us
    ppermute x1, starting transfers between devices, shards(): far_b = on_chip(lax.ppermute(own, ('gh', 'core'), beside))  6.01 us
  transfers between devices with their start and end apart: 9, of which 6 were waited for; matrix products, arithmetic and copies ran while one was open for 0% of the time, Pallas kernels for 6%

profile of v1, /device:TPU:1, one launch (start us, length us, event | category | flops | bytes accessed | tf_op | source)
XLA Modules:
  0.0 152.0 jit_solution(1504169673873690202)
XLA Ops:
  0.6 3.6 %shard_map.274 = f32[1024,128]{1,0:T(8,128)} custom-call(s32[4,32]{1,0:T(4,128)} %seed_ref.1, bf16[1024,512]{1,0:T(8,128)(2,1)} %constant.58.clone.th_ref.refs_2_, bf16[1024,512]{1,0:T(8,128)(2,1)} %constant.59.clone.tl_ref.refs_3_), custom_call_target="tpu_custom_call" | custom-call | tf_op jit(solution)/shard_map/pallas_call | solution.py:20
  4.2 22.1 %all-to-all-start = ((f32[512,2,128]{2,1,0:T(2,128)}), f32[512,2,128]{2,1,0:T(2,128)S(1)}, u32[]{:S(2)}, u32[]{:S(2)}) async-start(f32[512,2,128]{2,1,0:T(2,128)} %bitcast.28), calls=%async_computation | async-start | bytes 1048576 | tf_op jit(solution)/shard_map/all_to_all | solution.py:463
  26.4 21.9 %all-to-all-done = f32[512,2,128]{2,1,0:T(2,128)S(1)} async-done(((f32[512,2,128]{2,1,0:T(2,128)}), f32[512,2,128]{2,1,0:T(2,128)S(1)}, u32[]{:S(2)}, u32[]{:S(2)}) %all-to-all-start) | async-done | bytes 524320 | tf_op jit(solution)/shard_map/all_to_all | solution.py:463
  48.3 6.8 %shard_map.275 = f32[1280,128]{1,0:T(8,128)} custom-call(s32[1]{0:T(128)} %bitcast.refs_0_, f32[3]{0:T(128)} %refs_1_.1, f32[3]{0:T(128)} %refs_2_.3, f32[1024,128]{1,0:T(8,128)S(1)} %bitcast.20, bf16[512,512]{1,0:T(8,128)(2,1)} %constant.60.clone.refs_4_, bf16[512,512]{1,0:T(8,128)(2,1)} %constant.61.clone.refs_5_, ...), custom_call_target="tpu_custom_call" | custom-call | tf_op jit(solution)/shard_map/pallas_call | solution.py:20
  55.1 9.8 %all-to-all-start.1 = ((f32[256,1,640]{2,1,0:T(1,128)}), f32[256,1,640]{2,1,0:T(1,128)S(1)}, u32[]{:S(2)}, u32[]{:S(2)}) async-start(f32[256,1,640]{2,1,0:T(1,128)} %bitcast.25), calls=%async_computation.1 | async-start | bytes 1310720 | tf_op jit(solution)/shard_map/all_to_all | solution.py:463
  64.9 2.7 %shard_map.276 = (f32[128,1024]{1,0:T(8,128)}, f32[32,1024]{1,0:T(8,128)}, f32[32,1024]{1,0:T(8,128)}) custom-call(s32[1]{0:T(128)} %bitcast.refs_0_, f32[128,1024]{1,0:T(8,128)} %bitcast.29, s32[3,256]{1,0:T(4,128)} %refs_2_.4, f32[1,256]{1,0:T(1,128)} %bitcast.30, f32[128,1024]{1,0:T(8,128)} %bitcast.26), custom_call_target="tpu_custom_call" | custom-call | tf_op jit(solution)/shard_map/pallas_call | solution.py:20
  67.7 1.6 %collective-permute-start = (f32[32,1024]{1,0:T(8,128)}, f32[32,1024]{1,0:T(8,128)S(1)}, u32[]{:S(2)}, u32[]{:S(2)}) collective-permute-start(f32[32,1024]{1,0:T(8,128)} %get-tuple-element.23), channel_id=1, source_target_pairs={{0,16},{16,32},{32,48},{48,64},{64,80},{80,96},{96,112},{112,128},... | collective-permute-start | bytes 393224 | tf_op jit(solution)/shard_map/ppermute | solution.py:441
  69.3 1.3 collective-permute-start.1
  70.6 9.7 %collective-permute-done.refs_2_ = f32[32,1024]{1,0:T(8,128)S(1)} collective-permute-done((f32[32,1024]{1,0:T(8,128)}, f32[32,1024]{1,0:T(8,128)S(1)}, u32[]{:S(2)}, u32[]{:S(2)}) %collective-permute-start) | collective-permute-done | bytes 131104 | tf_op jit(solution)/shard_map/ppermute | solution.py:441
  80.3 2.1 %collective-permute-done.1.refs_3_ = f32[32,1024]{1,0:T(8,128)S(1)} collective-permute-done((f32[32,1024]{1,0:T(8,128)}, f32[32,1024]{1,0:T(8,128)S(1)}, u32[]{:S(2)}, u32[]{:S(2)}) %collective-permute-start.1) | collective-permute-done | bytes 131104 | tf_op jit(solution)/shard_map/ppermute | solution.py:442
  83.0 3.0 %shard_map.277 = (f32[160,1024]{1,0:T(8,128)}, f32[160,1024]{1,0:T(8,128)}, f32[240,1024]{1,0:T(8,128)}, f32[240,1024]{1,0:T(8,128)}) custom-call(f32[128,1024]{1,0:T(8,128)} %bitcast.27, f32[128,1024]{1,0:T(8,128)} %get-tuple-element.22.refs_1_, f32[32,1024]{1,0:T(8,128)} %copy-done.3, f32[32,1024]{1,0:T(8,128)} %copy-done.4), custom_call_target="tpu_custom_call" | custom-call | tf_op jit(solution)/shard_map/pallas_call | solution.py:20
  86.0 3.0 %collective-permute-start.5 = (f32[240,1024]{1,0:T(8,128)}, f32[240,1024]{1,0:T(8,128)S(1)}, u32[]{:S(2)}, u32[]{:S(2)}) collective-permute-start(f32[240,1024]{1,0:T(8,128)} %get-tuple-element.31), channel_id=1, source_target_pairs={{0,1},{1,2},{2,3},{3,4},{4,5},{5,6},{6,7},{7,8},{8,9},{9,10},{10,1... | collective-permute-start | bytes 2949128 | tf_op jit(solution)/shard_map/ppermute | solution.py:441
  89.1 1.9 %collective-permute-start.6 = (f32[240,1024]{1,0:T(8,128)}, f32[240,1024]{1,0:T(8,128)S(1)}, u32[]{:S(2)}, u32[]{:S(2)}) collective-permute-start(f32[240,1024]{1,0:T(8,128)} %get-tuple-element.25.refs_4_), channel_id=1, source_target_pairs={{1,0},{2,1},{3,2},{4,3},{5,4},{6,5},{7,6},{8,7},{9,8},{10,9},{11,1... | collective-permute-start | bytes 2949128 | tf_op jit(solution)/shard_map/ppermute | solution.py:442
  91.1 3.5 %shard_map.278 = (f32[320,512]{1,0:T(8,128)}, f32[160,512]{1,0:T(8,128)}, f32[160,512]{1,0:T(8,128)}) custom-call(s32[1]{0:T(128)} %bitcast.refs_0_, f32[1280,128]{1,0:T(8,128)S(1)} %bitcast.19, bf16[1024,512]{1,0:T(8,128)(2,1)} %constant.58.clone.th_ref.refs_2_, bf16[1024,512]{1,0:T(8,128)(2,1)} %constant.59.clone.tl_ref.refs_3_, ...), custom_call_target="tpu_custom_call" | custom-call | tf_op jit(solution)/shard_map/pallas_call | solution.py:20
  94.5 1.9 %collective-permute-start.2 = (f32[320,512]{1,0:T(8,128)}, f32[320,512]{1,0:T(8,128)S(1)}, u32[]{:S(2)}, u32[]{:S(2)}) collective-permute-start(f32[320,512]{1,0:T(8,128)} %get-tuple-element.26.refs_1_), channel_id=1, source_target_pairs={{0,1},{1,0},{2,3},{3,2},{4,5},{5,4},{6,7},{7,6},{8,9},{9,8},{10,11... | collective-permute-start | bytes 1966088 | tf_op jit(solution)/shard_map/ppermute | solution.py:510
  96.5 1.3 collective-permute-start.3
  97.8 6.0 %collective-permute-start.4 = (f32[160,512]{1,0:T(8,128)}, f32[160,512]{1,0:T(8,128)S(1)}, u32[]{:S(2)}, u32[]{:S(2)}) collective-permute-start(f32[160,512]{1,0:T(8,128)} %get-tuple-element.28), channel_id=1, source_target_pairs={{1,2},{3,4},{5,6},{7,8},{9,10},{11,12},{13,14},{2,1},{4,3},{6,5},{... | collective-permute-start | bytes 983048 | tf_op jit(solution)/shard_map/ppermute | solution.py:509
  103.8 4.3 %collective-permute-done.6.refs_8_ = f32[240,1024]{1,0:T(8,128)S(1)} collective-permute-done((f32[240,1024]{1,0:T(8,128)}, f32[240,1024]{1,0:T(8,128)S(1)}, u32[]{:S(2)}, u32[]{:S(2)}) %collective-permute-start.6) | collective-permute-done | bytes 983072 | tf_op jit(solution)/shard_map/ppermute | solution.py:442
  108.4 3.4 %collective-permute-done.4.refs_4_ = f32[160,512]{1,0:T(8,128)S(1)} collective-permute-done((f32[160,512]{1,0:T(8,128)}, f32[160,512]{1,0:T(8,128)S(1)}, u32[]{:S(2)}, u32[]{:S(2)}) %collective-permute-start.4) | collective-permute-done | bytes 327712 | tf_op jit(solution)/shard_map/ppermute | solution.py:509
  111.8 1.1 copy-done.2
  112.8 5.3 %shard_map.279 = (f32[128,1024]{1,0:T(8,128)}, f32[128,1024]{1,0:T(8,128)S(1)}, f32[128,1024]{1,0:T(8,128)S(1)}, f32[128,1024]{1,0:T(8,128)S(1)}, f32[128,1024]{...) custom-call(s32[1]{0:T(128)} %bitcast.refs_0_, f32[320,512]{1,0:T(8,128)S(1)} %copy-done.2, ...), custom_call_target="tpu_custom_call" | custom-call | tf_op jit(solution)/shard_map/pallas_call | solution.py:20
  118.2 17.7 %all_to_all.38 = f32[32,1,128]{2,1,0:T(1,128)S(1)} all-to-all(f32[32,1,128]{2,1,0:T(1,128)S(1)} %bitcast.24), channel_id=1, replica_groups=mesh['gx'=32,'gh'=8,'core'=2] {'gx'}, dimensions={0} | all-to-all | bytes 32768 | tf_op jit(solution)/shard_map/all_to_all | solution.py:529
  135.9 14.7 %all_to_all.39 = f32[16,1,128]{2,1,0:T(1,128)S(1)} all-to-all(f32[16,1,128]{2,1,0:T(1,128)S(1)} %bitcast.23), channel_id=1, replica_groups=mesh['gx'=32,'gh'=8,'core'=2] {'gh','core'}, dimensions={0} | all-to-all | bytes 16384 | tf_op jit(solution)/shard_map/all_to_all | solution.py:531
  150.6 1.5 shard_map.281
  (14 shorter events, 1.0 us)
Async XLA Ops:
  4.2 44.1 %all-to-all-start = ((f32[512,2,128]{2,1,0:T(2,128)}), f32[512,2,128]{2,1,0:T(2,128)S(1)}, u32[]{:S(2)}, u32[]{:S(2)}) async-start(f32[512,2,128]{2,1,0:T(2,128)} %bitcast.28), calls=%async_computation | async-start | bytes 1048576 | tf_op jit(solution)/shard_map/all_to_all | solution.py:463
  55.1 35.9 %all-to-all-start.1 = ((f32[256,1,640]{2,1,0:T(1,128)}), f32[256,1,640]{2,1,0:T(1,128)S(1)}, u32[]{:S(2)}, u32[]{:S(2)}) async-start(f32[256,1,640]{2,1,0:T(1,128)} %bitcast.25), calls=%async_computation.1 | async-start | bytes 1310720 | tf_op jit(solution)/shard_map/all_to_all | solution.py:463
  67.7 12.6 %collective-permute-start = (f32[32,1024]{1,0:T(8,128)}, f32[32,1024]{1,0:T(8,128)S(1)}, u32[]{:S(2)}, u32[]{:S(2)}) collective-permute-start(f32[32,1024]{1,0:T(8,128)} %get-tuple-element.23), channel_id=1, source_target_pairs={{0,16},{16,32},{32,48},{48,64},{64,80},{80,96},{96,112},{112,128},... | collective-permute-start | bytes 393224 | tf_op jit(solution)/shard_map/ppermute | solution.py:441
  69.3 13.1 %collective-permute-start.1 = (f32[32,1024]{1,0:T(8,128)}, f32[32,1024]{1,0:T(8,128)S(1)}, u32[]{:S(2)}, u32[]{:S(2)}) collective-permute-start(f32[32,1024]{1,0:T(8,128)} %get-tuple-element.24), channel_id=1, source_target_pairs={{16,0},{32,16},{48,32},{64,48},{80,64},{96,80},{112,96},{128,112},... | collective-permute-start | bytes 393224 | tf_op jit(solution)/shard_map/ppermute | solution.py:442
  80.3 2.1 %copy-start.3 = (f32[32,1024]{1,0:T(8,128)}, f32[32,1024]{1,0:T(8,128)S(1)}, u32[]{:S(2)}) copy-start(f32[32,1024]{1,0:T(8,128)S(1)} %collective-permute-done.refs_2_) | copy-start | bytes 393220
  82.4 0.7 copy-start.4
  86.0 17.7 %collective-permute-start.5 = (f32[240,1024]{1,0:T(8,128)}, f32[240,1024]{1,0:T(8,128)S(1)}, u32[]{:S(2)}, u32[]{:S(2)}) collective-permute-start(f32[240,1024]{1,0:T(8,128)} %get-tuple-element.31), channel_id=1, source_target_pairs={{0,1},{1,2},{2,3},{3,4},{4,5},{5,6},{6,7},{7,8},{8,9},{9,10},{10,1... | collective-permute-start | bytes 2949128 | tf_op jit(solution)/shard_map/ppermute | solution.py:441
  89.1 19.0 %collective-permute-start.6 = (f32[240,1024]{1,0:T(8,128)}, f32[240,1024]{1,0:T(8,128)S(1)}, u32[]{:S(2)}, u32[]{:S(2)}) collective-permute-start(f32[240,1024]{1,0:T(8,128)} %get-tuple-element.25.refs_4_), channel_id=1, source_target_pairs={{1,0},{2,1},{3,2},{4,3},{5,4},{6,5},{7,6},{8,7},{9,8},{10,9},{11,1... | collective-permute-start | bytes 2949128 | tf_op jit(solution)/shard_map/ppermute | solution.py:442
  91.0 20.7 %copy-start = (f32[160,1024]{1,0:T(8,128)S(1)}, f32[160,1024]{1,0:T(8,128)}, u32[]{:S(2)}) copy-start(f32[160,1024]{1,0:T(8,128)} %get-tuple-element.29.refs_5_) | copy-start | bytes 1966084
  91.0 20.7 %copy-start.1 = (f32[160,1024]{1,0:T(8,128)S(1)}, f32[160,1024]{1,0:T(8,128)}, u32[]{:S(2)}) copy-start(f32[160,1024]{1,0:T(8,128)} %get-tuple-element.30.refs_6_) | copy-start | bytes 1966084
  94.5 17.2 %collective-permute-start.2 = (f32[320,512]{1,0:T(8,128)}, f32[320,512]{1,0:T(8,128)S(1)}, u32[]{:S(2)}, u32[]{:S(2)}) collective-permute-start(f32[320,512]{1,0:T(8,128)} %get-tuple-element.26.refs_1_), channel_id=1, source_target_pairs={{0,1},{1,0},{2,3},{3,2},{4,5},{5,4},{6,7},{7,6},{8,9},{9,8},{10,11... | collective-permute-start | bytes 1966088 | tf_op jit(solution)/shard_map/ppermute | solution.py:510
  96.5 11.9 %collective-permute-start.3 = (f32[160,512]{1,0:T(8,128)}, f32[160,512]{1,0:T(8,128)S(1)}, u32[]{:S(2)}, u32[]{:S(2)}) collective-permute-start(f32[160,512]{1,0:T(8,128)} %get-tuple-element.27), channel_id=1, source_target_pairs={{0,2},{2,4},{4,6},{6,8},{8,10},{10,12},{12,14},{3,1},{5,3},{7,5},{... | collective-permute-start | bytes 983048 | tf_op jit(solution)/shard_map/ppermute | solution.py:508
  97.8 14.0 %collective-permute-start.4 = (f32[160,512]{1,0:T(8,128)}, f32[160,512]{1,0:T(8,128)S(1)}, u32[]{:S(2)}, u32[]{:S(2)}) collective-permute-start(f32[160,512]{1,0:T(8,128)} %get-tuple-element.28), channel_id=1, source_target_pairs={{1,2},{3,4},{5,6},{7,8},{9,10},{11,12},{13,14},{2,1},{4,3},{6,5},{... | collective-permute-start | bytes 983048 | tf_op jit(solution)/shard_map/ppermute | solution.py:509
  111.8 1.1 copy-start.2
